TPU v7x, 256 devices: a whole 4x4x8 slice. The times are simulated.
256 devices in a mesh: prow: 32 (over y, z), pcol: 8 (over x, core).
Axes of the slice: x: 4, y: 4, z: 8, core: 2. Of those that a mesh axis runs over, the one named last changes fastest.
Arguments:
- right_side: bfloat16 [32, 6, 128, 256], P('prow'), may hold values from -6 to 6
- lower_inverse: bfloat16 [32, 6, 256, 256], P('prow'), as said below
- upper_inverse: bfloat16 [32, 6, 256, 256], P('prow'), as said below
- lower_blocks: bfloat16 [32, 5, 48, 256, 256], P('prow', None, 'pcol'), may hold values from -0.0546875 to 0.0546875
- lower_sources: int32 [32, 5, 48], P('prow', None, 'pcol'), may hold values from 0 to 159, as said below
- lower_counts: int32 [32, 5, 8], P('prow', None, 'pcol'), may hold values from 1 to 6, as said below
- upper_blocks: bfloat16 [32, 5, 48, 256, 256], P('prow', None, 'pcol'), may hold values from -0.0546875 to 0.0546875
- upper_sources: int32 [32, 5, 48], P('prow', None, 'pcol'), may hold values from 32 to 191, as said below
- upper_counts: int32 [32, 5, 8], P('prow', None, 'pcol'), may hold values from 1 to 6, as said below
Outputs:
- solution: bfloat16 [32, 6, 128, 256], P('prow')
Inputs may be any that keep to these rules, and one draw needn't show every extreme that they name: `lower_sources`: entry [r, l, c] names supernode v * 32 + p of a level v below l + 1, with p % (8) == c // 6; entries may repeat. `upper_sources`: entry [r, l, c] names supernode v * 32 + p of a level v above l, with p % (8) == c // 6; entries may repeat. `lower_counts`: entry [r, l, g] is how many of the 6 slots of group g are live; the live ones come first. `upper_counts`: entry [r, l, g] is how many of the 6 slots of group g are live; the live ones come first. `lower_inverse`: each block is lower triangular. `upper_inverse`: each block is upper triangular.
All inputs are finite; a program needn't handle non-finite values.
Results may differ from a plain program's by a relative error of at most 0.02.
Values may be sent and summed in bfloat16 or wider, within the bound.
No kernel may reach another device: no remote copies, remote signals or barrier semaphores. Data moves between devices by JAX's collectives and lax.ppermute only.
A program may use at most 64 MiB of HBM per device.

v0:
```python
import jax
import jax.numpy as jnp
from jax import lax
from jax.sharding import PartitionSpec as P


def pick_sources(sources, count, store, width, ncol):
    group = store.shape[1]
    flat = store.reshape(store.shape[0] * group, store.shape[2], store.shape[3])
    position = sources // width * group + sources % width // ncol
    picked = flat[position]
    live = jnp.arange(sources.shape[0], dtype=jnp.int32) < count
    return jnp.where(live[:, None, None], picked, jnp.zeros_like(picked))


def contract(picked, blocks):
    return lax.dot_general(
        picked, blocks, (((0, 2), (0, 2)), ((), ())), preferred_element_type=jnp.float32
    )


def apply_inverse(residual, inverse):
    product = lax.dot_general(
        residual, inverse, (((1,), (1,)), ((), ())), preferred_element_type=jnp.float32
    )
    return product.astype(jnp.bfloat16)


def solve_level(right, inverse, blocks, sources, count, store):
    width = lax.axis_size("prow")
    ncol = lax.axis_size("pcol")
    picked = pick_sources(sources, count, store, width, ncol)
    total = lax.psum(contract(picked, blocks), "pcol")
    residual = (right.astype(jnp.float32) - total).astype(jnp.bfloat16)
    return apply_inverse(residual, inverse)


def spread(solved):
    ncol = lax.axis_size("pcol")
    column = lax.axis_index("pcol")
    whole = lax.all_gather(solved[None], "prow", axis=0, tiled=True)
    whole = whole.reshape(whole.shape[0] // ncol, ncol, whole.shape[1], whole.shape[2])
    return lax.dynamic_index_in_dim(whole, column, 1, keepdims=False)


def shards(
    right_side,
    lower_inverse,
    upper_inverse,
    lower_blocks,
    lower_sources,
    lower_counts,
    upper_blocks,
    upper_sources,
    upper_counts,
):
    group = lax.axis_size("prow") // lax.axis_size("pcol")
    levels = right_side.shape[1]
    shape = (levels, group, right_side.shape[2], right_side.shape[3])
    forward_store = jnp.zeros(shape, jnp.bfloat16)
    forward_own = []
    for level in range(levels):
        if level == 0:
            solved = apply_inverse(right_side[0, 0], lower_inverse[0, 0])
        else:
            solved = solve_level(
                right_side[0, level],
                lower_inverse[0, level],
                lower_blocks[0, level - 1],
                lower_sources[0, level - 1],
                lower_counts[0, level - 1, 0],
                forward_store,
            )
        forward_own.append(solved)
        if level + 1 < levels:
            forward_store = forward_store.at[level].set(spread(solved))
    backward_store = jnp.zeros(shape, jnp.bfloat16)
    backward_own = [None] * levels
    for level in range(levels - 1, -1, -1):
        if level == levels - 1:
            solved = apply_inverse(forward_own[level], upper_inverse[0, level])
        else:
            solved = solve_level(
                forward_own[level],
                upper_inverse[0, level],
                upper_blocks[0, level],
                upper_sources[0, level],
                upper_counts[0, level, 0],
                backward_store,
            )
        backward_own[level] = solved
        if level > 0:
            backward_store = backward_store.at[level].set(spread(solved))
    return jnp.stack(backward_own)[None]


def solution(mesh):
    in_specs = (
        P("prow", None, None, None),
        P("prow", None, None, None),
        P("prow", None, None, None),
        P("prow", None, "pcol", None, None),
        P("prow", None, "pcol"),
        P("prow", None, "pcol"),
        P("prow", None, "pcol", None, None),
        P("prow", None, "pcol"),
        P("prow", None, "pcol"),
    )
    out_specs = P("prow", None, None, None)
    return jax.shard_map(shards, mesh=mesh, in_specs=in_specs, out_specs=out_specs, check_vma=False)
```

profile of v0, /device:TPU:8, one launch (start us, length us, event | category | flops | bytes accessed | tf_op | source)
XLA Modules:
  0.0 1472.5 jit_solution(6980355928719453003)
XLA Ops:
  6.5 1.8 convolution_convert_fusion.11
  8.4 1.5 fusion.124
  9.9 0.6 iota_compare_fusion.7
  10.6 1.4 fusion.107
  12.0 77.6 %all-gather.21.cloned.1.call-done = bf16[4096,256]{1,0:T(8,128)(2,1)} async-done(((bf16[128,256]{1,0:T(8,128)(2,1)}), bf16[4096,256]{1,0:T(8,128)(2,1)}) %all-gather.21.cloned.1.call-update) | async-done | bytes 2097168 | tf_op jit(solution)/shard_map/all_gather | solution.py:41
  89.6 1.0 dynamic-slice_bitcast_fusion.1
  91.3 2.2 convolution_bitcast_fusion.9
  93.6 62.8 %all-reduce.13.cloned.1.call-done = f32[128,256]{1,0:T(8,128)} async-done(((f32[128,256]{1,0:T(8,128)}), f32[128,256]{1,0:T(8,128)}) %all-reduce.13.cloned.1.call-update) | async-done | bytes 131088 | tf_op jit(solution)/shard_map/psum | solution.py:33
  156.4 1.7 convolution_convert_fusion.10
  158.2 0.7 iota_compare_fusion.6
  159.0 76.3 %all-gather.23.cloned.1.call-done = bf16[4096,256]{1,0:T(8,128)(2,1)} async-done(((bf16[128,256]{1,0:T(8,128)(2,1)}), bf16[4096,256]{1,0:T(8,128)(2,1)}) %all-gather.23.cloned.1.call-update) | async-done | bytes 2097168 | tf_op jit(solution)/shard_map/all_gather | solution.py:41
  235.2 1.0 bitcast_dynamic-update-slice_fusion.7
  236.8 2.2 convolution_bitcast_fusion.8
  239.1 62.8 %all-reduce.15.cloned.1.call-done = f32[128,256]{1,0:T(8,128)} async-done(((f32[128,256]{1,0:T(8,128)}), f32[128,256]{1,0:T(8,128)}) %all-reduce.15.cloned.1.call-update) | async-done | bytes 131088 | tf_op jit(solution)/shard_map/psum | solution.py:33
  301.9 1.7 convolution_convert_fusion.9
  303.7 0.7 iota_compare_fusion.5
  304.4 75.8 %all-gather.25.cloned.1.call-done = bf16[4096,256]{1,0:T(8,128)(2,1)} async-done(((bf16[128,256]{1,0:T(8,128)(2,1)}), bf16[4096,256]{1,0:T(8,128)(2,1)}) %all-gather.25.cloned.1.call-update) | async-done | bytes 2097168 | tf_op jit(solution)/shard_map/all_gather | solution.py:41
  380.2 1.0 bitcast_dynamic-update-slice_fusion.6
  381.7 2.2 convolution_bitcast_fusion.7
  384.0 62.8 %all-reduce.17.cloned.1.call-done = f32[128,256]{1,0:T(8,128)} async-done(((f32[128,256]{1,0:T(8,128)}), f32[128,256]{1,0:T(8,128)}) %all-reduce.17.cloned.1.call-update) | async-done | bytes 131088 | tf_op jit(solution)/shard_map/psum | solution.py:33
  446.8 1.7 convolution_convert_fusion.8
  449.3 76.3 %all-gather.27.cloned.1.call-done = bf16[4096,256]{1,0:T(8,128)(2,1)} async-done(((bf16[128,256]{1,0:T(8,128)(2,1)}), bf16[4096,256]{1,0:T(8,128)(2,1)}) %all-gather.27.cloned.1.call-update) | async-done | bytes 2097168 | tf_op jit(solution)/shard_map/all_gather | solution.py:41
  525.6 1.0 bitcast_dynamic-update-slice_fusion.5
  527.2 2.2 convolution_bitcast_fusion.6
  529.4 62.8 %all-reduce.19.cloned.1.call-done = f32[128,256]{1,0:T(8,128)} async-done(((f32[128,256]{1,0:T(8,128)}), f32[128,256]{1,0:T(8,128)}) %all-reduce.19.cloned.1.call-update) | async-done | bytes 131088 | tf_op jit(solution)/shard_map/psum | solution.py:33
  592.2 1.7 convolution_convert_fusion.7
  594.0 1.1 iota_compare_fusion.8
  595.1 0.7 pad_clamp_fusion.5
  595.8 74.9 %all-gather.29.cloned.1.call-done = bf16[4096,256]{1,0:T(8,128)(2,1)} async-done(((bf16[128,256]{1,0:T(8,128)(2,1)}), bf16[4096,256]{1,0:T(8,128)(2,1)}) %all-gather.29.cloned.1.call-update) | async-done | bytes 2097168 | tf_op jit(solution)/shard_map/all_gather | solution.py:41
  670.7 1.0 bitcast_dynamic-update-slice_fusion.4
  672.3 2.2 convolution_bitcast_fusion.5
  674.5 62.8 %all-reduce.21.cloned.1.call-done = f32[128,256]{1,0:T(8,128)} async-done(((f32[128,256]{1,0:T(8,128)}), f32[128,256]{1,0:T(8,128)}) %all-reduce.21.cloned.1.call-update) | async-done | bytes 131088 | tf_op jit(solution)/shard_map/psum | solution.py:33
  737.4 1.9 convolution_convert_fusion.5
  739.3 0.7 fusion.123
  740.0 0.6 iota_compare_fusion.3
  740.6 0.6 pad_clamp_fusion.4
  741.3 74.9 %all-gather.31.cloned.1.call-done = bf16[4096,256]{1,0:T(8,128)(2,1)} async-done(((bf16[128,256]{1,0:T(8,128)(2,1)}), bf16[4096,256]{1,0:T(8,128)(2,1)}) %all-gather.31.cloned.1.call-update) | async-done | bytes 2097168 | tf_op jit(solution)/shard_map/all_gather | solution.py:41
  816.2 1.0 dynamic-slice_bitcast_fusion
  817.9 2.2 convolution_bitcast_fusion.4
  820.2 62.8 %all-reduce.23.cloned.1.call-done = f32[128,256]{1,0:T(8,128)} async-done(((f32[128,256]{1,0:T(8,128)}), f32[128,256]{1,0:T(8,128)}) %all-reduce.23.cloned.1.call-update) | async-done | bytes 131088 | tf_op jit(solution)/shard_map/psum | solution.py:33
  883.0 1.7 convolution_convert_fusion.4
  884.8 0.7 iota_compare_fusion.2
  885.5 75.9 %all-gather.33.cloned.1.call-done = bf16[4096,256]{1,0:T(8,128)(2,1)} async-done(((bf16[128,256]{1,0:T(8,128)(2,1)}), bf16[4096,256]{1,0:T(8,128)(2,1)}) %all-gather.33.cloned.1.call-update) | async-done | bytes 2097168 | tf_op jit(solution)/shard_map/all_gather | solution.py:41
  961.4 1.0 bitcast_dynamic-update-slice_fusion.3
  963.0 2.2 convolution_bitcast_fusion.3
  965.3 62.8 %all-reduce.25.cloned.1.call-done = f32[128,256]{1,0:T(8,128)} async-done(((f32[128,256]{1,0:T(8,128)}), f32[128,256]{1,0:T(8,128)}) %all-reduce.25.cloned.1.call-update) | async-done | bytes 131088 | tf_op jit(solution)/shard_map/psum | solution.py:33
  1028.1 1.7 convolution_convert_fusion.3
  1030.5 76.2 %all-gather.35.cloned.1.call-done = bf16[4096,256]{1,0:T(8,128)(2,1)} async-done(((bf16[128,256]{1,0:T(8,128)(2,1)}), bf16[4096,256]{1,0:T(8,128)(2,1)}) %all-gather.35.cloned.1.call-update) | async-done | bytes 2097168 | tf_op jit(solution)/shard_map/all_gather | solution.py:41
  1106.7 1.0 bitcast_dynamic-update-slice_fusion.2
  1108.3 2.2 convolution_bitcast_fusion.2
  1110.6 62.8 %all-reduce.27.cloned.1.call-done = f32[128,256]{1,0:T(8,128)} async-done(((f32[128,256]{1,0:T(8,128)}), f32[128,256]{1,0:T(8,128)}) %all-reduce.27.cloned.1.call-update) | async-done | bytes 131088 | tf_op jit(solution)/shard_map/psum | solution.py:33
  1173.4 1.7 convolution_convert_fusion.2
  1175.8 75.9 %all-gather.37.cloned.1.call-done = bf16[4096,256]{1,0:T(8,128)(2,1)} async-done(((bf16[128,256]{1,0:T(8,128)(2,1)}), bf16[4096,256]{1,0:T(8,128)(2,1)}) %all-gather.37.cloned.1.call-update) | async-done | bytes 2097168 | tf_op jit(solution)/shard_map/all_gather | solution.py:41
  1251.7 1.0 bitcast_dynamic-update-slice_fusion.1
  1253.2 2.2 convolution_bitcast_fusion.1
  1255.5 62.8 %all-reduce.29.cloned.1.call-done = f32[128,256]{1,0:T(8,128)} async-done(((f32[128,256]{1,0:T(8,128)}), f32[128,256]{1,0:T(8,128)}) %all-reduce.29.cloned.1.call-update) | async-done | bytes 131088 | tf_op jit(solution)/shard_map/psum | solution.py:33
  1318.3 1.7 convolution_convert_fusion.1
  1320.1 0.7 iota_compare_fusion.9
  1320.8 76.3 %all-gather.39.cloned.1.call-done = bf16[4096,256]{1,0:T(8,128)(2,1)} async-done(((bf16[128,256]{1,0:T(8,128)(2,1)}), bf16[4096,256]{1,0:T(8,128)(2,1)}) %all-gather.39.cloned.1.call-update) | async-done | bytes 2097168 | tf_op jit(solution)/shard_map/all_gather | solution.py:41
  1397.1 1.0 bitcast_dynamic-update-slice_fusion
  1398.7 2.2 convolution_bitcast_fusion
  1400.9 62.8 %all-reduce.31.cloned.1.call-done = f32[128,256]{1,0:T(8,128)} async-done(((f32[128,256]{1,0:T(8,128)}), f32[128,256]{1,0:T(8,128)}) %all-reduce.31.cloned.1.call-update) | async-done | bytes 131088 | tf_op jit(solution)/shard_map/psum | solution.py:33
  1463.7 1.1 fusion.1
  1465.0 0.7 copy-done.14
  (101 shorter events, 9.1 us)
Async XLA Ops:
  6.5 83.1 %all-gather.21.cloned.1.call-start = ((), (), s32[]{:S(2)}) async-start(), calls=%async_computation.10 | async-start | bytes 2162688 | tf_op jit(solution)/shard_map/all_gather | solution.py:41
  8.3 148.1 %all-reduce.13.cloned.1.call-start = ((), (), s32[]{:S(2)}) async-start(), calls=%async_computation | async-start | bytes 262144 | tf_op jit(solution)/shard_map/psum | solution.py:33
  90.6 65.9 %copy-start.1 = (bf16[1,6,256,256]{3,2,1,0:T(8,128)(2,1)S(1)}, bf16[1,6,256,256]{3,2,1,0:T(8,128)(2,1)}, u32[]{:S(2)}) copy-start(bf16[1,6,256,256]{3,2,1,0:T(8,128)(2,1)} %param.30) | copy-start | bytes 2359300
  90.6 65.8 %copy-start.12 = (bf16[1,6,128,256]{3,2,1,0:T(8,128)(2,1)S(1)}, bf16[1,6,128,256]{3,2,1,0:T(8,128)(2,1)}, u32[]{:S(2)}) copy-start(bf16[1,6,128,256]{3,2,1,0:T(8,128)(2,1)} %param.29) | copy-start | bytes 1179652
  93.6 141.7 %all-gather.23.cloned.1.call-start = ((), (), s32[]{:S(2)}) async-start(), calls=%async_computation.11 | async-start | bytes 2162688 | tf_op jit(solution)/shard_map/all_gather | solution.py:41
  158.2 143.7 %all-reduce.15.cloned.1.call-start = ((), (), s32[]{:S(2)}) async-start(), calls=%async_computation.1 | async-start | bytes 262144 | tf_op jit(solution)/shard_map/psum | solution.py:33
  239.0 141.2 %all-gather.25.cloned.1.call-start = ((), (), s32[]{:S(2)}) async-start(), calls=%async_computation.12 | async-start | bytes 2162688 | tf_op jit(solution)/shard_map/all_gather | solution.py:41
  303.6 143.2 %all-reduce.17.cloned.1.call-start = ((), (), s32[]{:S(2)}) async-start(), calls=%async_computation.2 | async-start | bytes 262144 | tf_op jit(solution)/shard_map/psum | solution.py:33
  383.9 141.7 %all-gather.27.cloned.1.call-start = ((), (), s32[]{:S(2)}) async-start(), calls=%async_computation.13 | async-start | bytes 2162688 | tf_op jit(solution)/shard_map/all_gather | solution.py:41
  448.6 143.7 %all-reduce.19.cloned.1.call-start = ((), (), s32[]{:S(2)}) async-start(), calls=%async_computation.3 | async-start | bytes 262144 | tf_op jit(solution)/shard_map/psum | solution.py:33
  529.3 208.0 %copy-start = (bf16[1,6,256,256]{3,2,1,0:T(8,128)(2,1)S(1)}, bf16[1,6,256,256]{3,2,1,0:T(8,128)(2,1)}, u32[]{:S(2)}) copy-start(bf16[1,6,256,256]{3,2,1,0:T(8,128)(2,1)} %param.31) | copy-start | bytes 2359300
  529.4 209.9 %copy-start.13 = (s32[1,5,1]{1,2,0:T(1,128)S(1)}, s32[1,5,1]{1,2,0:T(1,128)}, u32[]{:S(2)}) copy-start(s32[1,5,1]{1,2,0:T(1,128)} %param.37) | copy-start | bytes 64
  529.4 141.3 %all-gather.29.cloned.1.call-start = ((), (), s32[]{:S(2)}) async-start(), calls=%async_computation.14 | async-start | bytes 2162688 | tf_op jit(solution)/shard_map/all_gather | solution.py:41
  594.0 143.4 %all-reduce.21.cloned.1.call-start = ((), (), s32[]{:S(2)}) async-start(), calls=%async_computation.4 | async-start | bytes 262144 | tf_op jit(solution)/shard_map/psum | solution.py:33
  674.5 141.7 %all-gather.31.cloned.1.call-start = ((), (), s32[]{:S(2)}) async-start(), calls=%async_computation.15 | async-start | bytes 2162688 | tf_op jit(solution)/shard_map/all_gather | solution.py:41
  739.2 143.7 %all-reduce.23.cloned.1.call-start = ((), (), s32[]{:S(2)}) async-start(), calls=%async_computation.5 | async-start | bytes 262144 | tf_op jit(solution)/shard_map/psum | solution.py:33
  817.1 65.9 %copy-start.10 = (bf16[128,256]{1,0:T(8,128)(2,1)S(1)}, bf16[128,256]{1,0:T(8,128)(2,1)}, u32[]{:S(2)}) copy-start(bf16[128,256]{1,0:T(8,128)(2,1)} %convolution_convert_fusion.7) | copy-start | bytes 196612
  817.1 68.3 %copy-start.16 = (s32[6]{0:T(128)S(1)}, s32[6]{0:T(128)}, u32[]{:S(2)}) copy-start(s32[6]{0:T(128)} %get-tuple-element.147) | copy-start | bytes 76
  820.1 208.0 %copy-start.9 = (bf16[128,256]{1,0:T(8,128)(2,1)S(1)}, bf16[128,256]{1,0:T(8,128)(2,1)}, u32[]{:S(2)}) copy-start(bf16[128,256]{1,0:T(8,128)(2,1)} %convolution_convert_fusion.8) | copy-start | bytes 196612
  820.1 210.4 %copy-start.15 = (s32[6]{0:T(128)S(1)}, s32[6]{0:T(128)}, u32[]{:S(2)}) copy-start(s32[6]{0:T(128)} %get-tuple-element.148) | copy-start | bytes 76
  820.1 141.3 %all-gather.33.cloned.1.call-start = ((), (), s32[]{:S(2)}) async-start(), calls=%async_computation.16 | async-start | bytes 2162688 | tf_op jit(solution)/shard_map/all_gather | solution.py:41
  884.7 143.3 %all-reduce.25.cloned.1.call-start = ((), (), s32[]{:S(2)}) async-start(), calls=%async_computation.6 | async-start | bytes 262144 | tf_op jit(solution)/shard_map/psum | solution.py:33
  965.2 208.2 %copy-start.8 = (bf16[128,256]{1,0:T(8,128)(2,1)S(1)}, bf16[128,256]{1,0:T(8,128)(2,1)}, u32[]{:S(2)}) copy-start(bf16[128,256]{1,0:T(8,128)(2,1)} %convolution_convert_fusion.9) | copy-start | bytes 196612
  965.2 141.5 %all-gather.35.cloned.1.call-start = ((), (), s32[]{:S(2)}) async-start(), calls=%async_computation.17 | async-start | bytes 2162688 | tf_op jit(solution)/shard_map/all_gather | solution.py:41
  1029.8 143.5 %all-reduce.27.cloned.1.call-start = ((), (), s32[]{:S(2)}) async-start(), calls=%async_computation.7 | async-start | bytes 262144 | tf_op jit(solution)/shard_map/psum | solution.py:33
  1110.5 207.8 %copy-start.7 = (bf16[128,256]{1,0:T(8,128)(2,1)S(1)}, bf16[128,256]{1,0:T(8,128)(2,1)}, u32[]{:S(2)}) copy-start(bf16[128,256]{1,0:T(8,128)(2,1)} %convolution_convert_fusion.10) | copy-start | bytes 196612
  1110.5 141.2 %all-gather.37.cloned.1.call-start = ((), (), s32[]{:S(2)}) async-start(), calls=%async_computation.18 | async-start | bytes 2162688 | tf_op jit(solution)/shard_map/all_gather | solution.py:41
  1175.1 143.2 %all-reduce.29.cloned.1.call-start = ((), (), s32[]{:S(2)}) async-start(), calls=%async_computation.8 | async-start | bytes 262144 | tf_op jit(solution)/shard_map/psum | solution.py:33
  1255.4 208.3 %copy-start.6 = (bf16[128,256]{1,0:T(8,128)(2,1)S(1)}, bf16[128,256]{1,0:T(8,128)(2,1)}, u32[]{:S(2)}) copy-start(bf16[128,256]{1,0:T(8,128)(2,1)} %convolution_convert_fusion.11) | copy-start | bytes 196612
  1255.5 209.4 %copy-start.4 = (bf16[128,256]{1,0:T(8,128)(2,1)S(1)}, bf16[128,256]{1,0:T(8,128)(2,1)}, u32[]{:S(2)}) copy-start(bf16[128,256]{1,0:T(8,128)(2,1)} %convolution_convert_fusion.2) | copy-start | bytes 196612
  1255.5 209.4 %copy-start.3 = (bf16[128,256]{1,0:T(8,128)(2,1)S(1)}, bf16[128,256]{1,0:T(8,128)(2,1)}, u32[]{:S(2)}) copy-start(bf16[128,256]{1,0:T(8,128)(2,1)} %convolution_convert_fusion.3) | copy-start | bytes 196612
  1255.5 141.6 %all-gather.39.cloned.1.call-start = ((), (), s32[]{:S(2)}) async-start(), calls=%async_computation.19 | async-start | bytes 2162688 | tf_op jit(solution)/shard_map/all_gather | solution.py:41
  1320.1 144.8 %copy-start.5 = (bf16[128,256]{1,0:T(8,128)(2,1)S(1)}, bf16[128,256]{1,0:T(8,128)(2,1)}, u32[]{:S(2)}) copy-start(bf16[128,256]{1,0:T(8,128)(2,1)} %convolution_convert_fusion.1) | copy-start | bytes 196612
  1320.1 144.9 %copy-start.2 = (bf16[128,256]{1,0:T(8,128)(2,1)S(1)}, bf16[128,256]{1,0:T(8,128)(2,1)}, u32[]{:S(2)}) copy-start(bf16[128,256]{1,0:T(8,128)(2,1)} %convolution_convert_fusion.4) | copy-start | bytes 196612
  1320.1 144.9 %copy-start.11 = (bf16[128,256]{1,0:T(8,128)(2,1)S(1)}, bf16[128,256]{1,0:T(8,128)(2,1)}, u32[]{:S(2)}) copy-start(bf16[128,256]{1,0:T(8,128)(2,1)} %convolution_convert_fusion.5) | copy-start | bytes 196612
  1320.1 143.6 %all-reduce.31.cloned.1.call-start = ((), (), s32[]{:S(2)}) async-start(), calls=%async_computation.9 | async-start | bytes 262144 | tf_op jit(solution)/shard_map/psum | solution.py:33
  1465.0 0.7 copy-start.14
Sparse Core Ops, SparseCore 0:
  9.9 79.6 all-gather.20
  93.7 62.6 all-reduce.12
  159.4 75.8 all-gather.22
  239.1 62.6 all-reduce.14
  304.3 75.8 all-gather.24
  384.1 62.6 all-reduce.16
  449.7 75.8 all-gather.26
  529.5 62.6 all-reduce.18
  594.8 75.8 all-gather.28
  674.6 62.6 all-reduce.20
  740.3 75.8 all-gather.30
  820.2 62.7 all-reduce.22
  885.6 75.8 all-gather.32
  965.3 62.6 all-reduce.24
  1030.9 75.8 all-gather.34
  1110.6 62.6 all-reduce.26
  1175.8 75.8 all-gather.36
  1255.6 62.6 all-reduce.28
  1321.2 75.8 all-gather.38
  1401.0 62.6 all-reduce.30
where the time goes:
time: 1470 us
  waiting for transfers between devices  1390 us (95%)
  matrix products  40.5 us (3%)
  local copies, waits for them, and re-layouts  18.7 us (1%)
    all_gather x10, waiting for transfers between devices, spread(): whole = lax.all_gather(solved[None], 'prow', axis=0, tiled=True)  760 us
    psum x10, waiting for transfers between devices, solve_level(): total = lax.psum(contract(picked, blocks), 'pcol')  628 us
  transfers between devices with their start and end apart: 20, of which 20 were waited for; matrix products, arithmetic and copies ran while one was open for 1% of the time, Pallas kernels for 0%

commit v1 on v0

--- a/solution.py
+++ b/solution.py
@@ -38,7 +38,9 @@
 def spread(solved):
     ncol = lax.axis_size("pcol")
     column = lax.axis_index("pcol")
-    whole = lax.all_gather(solved[None], "prow", axis=0, tiled=True)
+    whole = jnp.concatenate(
+        lax.all_to_all(jnp.stack([solved[None]] * lax.axis_size("prow")), "prow", 0, 0), axis=0
+    )
     whole = whole.reshape(whole.shape[0] // ncol, ncol, whole.shape[1], whole.shape[2])
     return lax.dynamic_index_in_dim(whole, column, 1, keepdims=False)
 

time: 1470 us -> 1290 us (0.88)
  waiting for transfers between devices: 1390 us -> 1100 us
  starting transfers between devices: 0.8 us -> 104 us
    all_gather x10 -> x0, waiting for transfers between devices: 760 us -> none  [spread(): whole = lax.all_gather(solved[None], 'prow', axis=0, tiled=True)]
    all_to_all x0 -> x10, waiting for transfers between devices: none -> 452 us  [spread(): lax.all_to_all(jnp.stack([solved[None]] * lax.axis_size('prow')), 'prow',...]
    all_to_all x0 -> x10, starting transfers between devices: none -> 104 us  [spread(): lax.all_to_all(jnp.stack([solved[None]] * lax.axis_size('prow')), 'prow',...]
    psum x10, waiting for transfers between devices: 628 us -> 646 us  [solve_level(): total = lax.psum(contract(picked, blocks), 'pcol')]
where the time goes in v1:
time: 1290 us
  waiting for transfers between devices  1100 us (85%)
  starting transfers between devices  104 us (8%)
  matrix products  34.2 us (3%)
  local copies, waits for them, and re-layouts  32.5 us (3%)
  between operations  14.1 us (1%)
    psum x10, waiting for transfers between devices, solve_level(): total = lax.psum(contract(picked, blocks), 'pcol')  646 us
    all_to_all x10, waiting for transfers between devices, spread(): lax.all_to_all(jnp.stack([solved[None]] * lax.axis_size('prow')), 'prow',...  452 us
    all_to_all x10, starting transfers between devices, spread(): lax.all_to_all(jnp.stack([solved[None]] * lax.axis_size('prow')), 'prow',...  104 us
  transfers between devices with their start and end apart: 20, of which 20 were waited for; matrix products, arithmetic and copies ran while one was open for 1% of the time, Pallas kernels for 0%

profile of v1, /device:TPU:8, one launch (start us, length us, event | category | flops | bytes accessed | tf_op | source)
XLA Modules:
  0.0 1290.4 jit_solution(15998934381836157143)
XLA Ops:
  6.5 1.1 convolution_convert_fusion.11
  7.7 1.6 stack.51
  9.3 11.8 all-to-all-start
  23.1 45.5 %all-to-all-done = bf16[32,1,128,256]{3,2,1,0:T(8,128)(2,1)S(1)} async-done(((bf16[32,1,128,256]{3,2,1,0:T(8,128)(2,1)}), bf16[32,1,128,256]{3,2,1,0:T(8,128)(2,1)S(1)}, u32[]{:S(2)}, u32[]{:S(2)}) %all-to-all-start) | async-done | bytes 2097184 | tf_op jit(solution)/shard_map/all_to_all | solution.py:42
  69.4 2.2 convolution_bitcast_fusion.9
  71.6 64.2 %all-reduce.13.cloned.1.call-done = f32[128,256]{1,0:T(8,128)} async-done(((f32[128,256]{1,0:T(8,128)}), f32[128,256]{1,0:T(8,128)}) %all-reduce.13.cloned.1.call-update) | async-done | bytes 131088 | tf_op jit(solution)/shard_map/psum | solution.py:33
  135.9 1.1 convolution_convert_fusion.10
  137.0 1.6 stack.52
  138.5 10.2 all-to-all-start.1
  149.5 45.2 %all-to-all-done.1 = bf16[32,1,128,256]{3,2,1,0:T(8,128)(2,1)} async-done(((bf16[32,1,128,256]{3,2,1,0:T(8,128)(2,1)}), bf16[32,1,128,256]{3,2,1,0:T(8,128)(2,1)}, u32[]{:S(2)}, u32[]{:S(2)}) %all-to-all-start.1) | async-done | bytes 2097184 | tf_op jit(solution)/shard_map/all_to_all | solution.py:42
  194.8 1.0 bitcast_dynamic-update-slice_fusion.7
  196.3 2.2 convolution_bitcast_fusion.8
  198.5 64.6 %all-reduce.15.cloned.1.call-done = f32[128,256]{1,0:T(8,128)} async-done(((f32[128,256]{1,0:T(8,128)}), f32[128,256]{1,0:T(8,128)}) %all-reduce.15.cloned.1.call-update) | async-done | bytes 131088 | tf_op jit(solution)/shard_map/psum | solution.py:33
  263.1 1.1 convolution_convert_fusion.9
  264.2 1.6 stack.53
  265.8 10.2 all-to-all-start.2
  276.7 45.3 %all-to-all-done.2 = bf16[32,1,128,256]{3,2,1,0:T(8,128)(2,1)} async-done(((bf16[32,1,128,256]{3,2,1,0:T(8,128)(2,1)}), bf16[32,1,128,256]{3,2,1,0:T(8,128)(2,1)}, u32[]{:S(2)}, u32[]{:S(2)}) %all-to-all-start.2) | async-done | bytes 2097184 | tf_op jit(solution)/shard_map/all_to_all | solution.py:42
  323.6 2.2 convolution_bitcast_fusion.7
  325.8 64.6 %all-reduce.17.cloned.1.call-done = f32[128,256]{1,0:T(8,128)} async-done(((f32[128,256]{1,0:T(8,128)}), f32[128,256]{1,0:T(8,128)}) %all-reduce.17.cloned.1.call-update) | async-done | bytes 131088 | tf_op jit(solution)/shard_map/psum | solution.py:33
  390.4 1.1 convolution_convert_fusion.8
  391.5 1.6 stack.54
  393.1 10.2 all-to-all-start.3
  404.0 45.3 %all-to-all-done.3 = bf16[32,1,128,256]{3,2,1,0:T(8,128)(2,1)} async-done(((bf16[32,1,128,256]{3,2,1,0:T(8,128)(2,1)}), bf16[32,1,128,256]{3,2,1,0:T(8,128)(2,1)}, u32[]{:S(2)}, u32[]{:S(2)}) %all-to-all-start.3) | async-done | bytes 2097184 | tf_op jit(solution)/shard_map/all_to_all | solution.py:42
  450.8 2.2 convolution_bitcast_fusion.6
  453.1 64.6 %all-reduce.19.cloned.1.call-done = f32[128,256]{1,0:T(8,128)} async-done(((f32[128,256]{1,0:T(8,128)}), f32[128,256]{1,0:T(8,128)}) %all-reduce.19.cloned.1.call-update) | async-done | bytes 131088 | tf_op jit(solution)/shard_map/psum | solution.py:33
  517.7 1.1 convolution_convert_fusion.7
  518.8 1.6 stack.55
  520.4 10.2 all-to-all-start.4
  531.3 45.2 %all-to-all-done.4 = bf16[32,1,128,256]{3,2,1,0:T(8,128)(2,1)} async-done(((bf16[32,1,128,256]{3,2,1,0:T(8,128)(2,1)}), bf16[32,1,128,256]{3,2,1,0:T(8,128)(2,1)}, u32[]{:S(2)}, u32[]{:S(2)}) %all-to-all-start.4) | async-done | bytes 2097184 | tf_op jit(solution)/shard_map/all_to_all | solution.py:42
  577.5 1.3 gather_fusion.4
  578.9 2.3 convolution_bitcast_fusion.5
  581.2 64.6 %all-reduce.21.cloned.1.call-done = f32[128,256]{1,0:T(8,128)} async-done(((f32[128,256]{1,0:T(8,128)}), f32[128,256]{1,0:T(8,128)}) %all-reduce.21.cloned.1.call-update) | async-done | bytes 131088 | tf_op jit(solution)/shard_map/psum | solution.py:33
  645.8 1.2 convolution_convert_fusion.5
  647.0 1.6 stack.56
  648.6 10.3 all-to-all-start.5
  659.6 1.2 iota_compare_fusion.3
  660.9 44.0 %all-to-all-done.5 = bf16[32,1,128,256]{3,2,1,0:T(8,128)(2,1)S(1)} async-done(((bf16[32,1,128,256]{3,2,1,0:T(8,128)(2,1)}), bf16[32,1,128,256]{3,2,1,0:T(8,128)(2,1)S(1)}, u32[]{:S(2)}, u32[]{:S(2)}) %all-to-all-start.5) | async-done | bytes 2097184 | tf_op jit(solution)/shard_map/all_to_all | solution.py:42
  705.7 2.2 convolution_bitcast_fusion.4
  707.9 64.5 %all-reduce.23.cloned.1.call-done = f32[128,256]{1,0:T(8,128)} async-done(((f32[128,256]{1,0:T(8,128)}), f32[128,256]{1,0:T(8,128)}) %all-reduce.23.cloned.1.call-update) | async-done | bytes 131088 | tf_op jit(solution)/shard_map/psum | solution.py:33
  772.4 1.1 convolution_convert_fusion.4
  773.5 1.6 stack.57
  775.1 10.3 all-to-all-start.6
  786.2 45.2 %all-to-all-done.6 = bf16[32,1,128,256]{3,2,1,0:T(8,128)(2,1)} async-done(((bf16[32,1,128,256]{3,2,1,0:T(8,128)(2,1)}), bf16[32,1,128,256]{3,2,1,0:T(8,128)(2,1)}, u32[]{:S(2)}, u32[]{:S(2)}) %all-to-all-start.6) | async-done | bytes 2097184 | tf_op jit(solution)/shard_map/all_to_all | solution.py:42
  833.0 2.2 convolution_bitcast_fusion.3
  835.2 64.6 %all-reduce.25.cloned.1.call-done = f32[128,256]{1,0:T(8,128)} async-done(((f32[128,256]{1,0:T(8,128)}), f32[128,256]{1,0:T(8,128)}) %all-reduce.25.cloned.1.call-update) | async-done | bytes 131088 | tf_op jit(solution)/shard_map/psum | solution.py:33
  899.8 1.1 convolution_convert_fusion.3
  900.9 1.6 stack.58
  902.5 10.2 all-to-all-start.7
  913.4 45.3 %all-to-all-done.7 = bf16[32,1,128,256]{3,2,1,0:T(8,128)(2,1)} async-done(((bf16[32,1,128,256]{3,2,1,0:T(8,128)(2,1)}), bf16[32,1,128,256]{3,2,1,0:T(8,128)(2,1)}, u32[]{:S(2)}, u32[]{:S(2)}) %all-to-all-start.7) | async-done | bytes 2097184 | tf_op jit(solution)/shard_map/all_to_all | solution.py:42
  960.3 2.2 convolution_bitcast_fusion.2
  962.5 64.6 %all-reduce.27.cloned.1.call-done = f32[128,256]{1,0:T(8,128)} async-done(((f32[128,256]{1,0:T(8,128)}), f32[128,256]{1,0:T(8,128)}) %all-reduce.27.cloned.1.call-update) | async-done | bytes 131088 | tf_op jit(solution)/shard_map/psum | solution.py:33
  1027.1 1.1 convolution_convert_fusion.2
  1028.2 1.6 stack.59
  1029.8 10.2 all-to-all-start.8
  1040.7 45.3 %all-to-all-done.8 = bf16[32,1,128,256]{3,2,1,0:T(8,128)(2,1)} async-done(((bf16[32,1,128,256]{3,2,1,0:T(8,128)(2,1)}), bf16[32,1,128,256]{3,2,1,0:T(8,128)(2,1)}, u32[]{:S(2)}, u32[]{:S(2)}) %all-to-all-start.8) | async-done | bytes 2097184 | tf_op jit(solution)/shard_map/all_to_all | solution.py:42
  1087.5 2.2 convolution_bitcast_fusion.1
  1089.8 64.6 %all-reduce.29.cloned.1.call-done = f32[128,256]{1,0:T(8,128)} async-done(((f32[128,256]{1,0:T(8,128)}), f32[128,256]{1,0:T(8,128)}) %all-reduce.29.cloned.1.call-update) | async-done | bytes 131088 | tf_op jit(solution)/shard_map/psum | solution.py:33
  1154.3 1.1 convolution_convert_fusion.1
  1155.4 1.6 stack.60
  1157.0 10.2 all-to-all-start.9
  1167.9 45.3 %all-to-all-done.9 = bf16[32,1,128,256]{3,2,1,0:T(8,128)(2,1)} async-done(((bf16[32,1,128,256]{3,2,1,0:T(8,128)(2,1)}), bf16[32,1,128,256]{3,2,1,0:T(8,128)(2,1)}, u32[]{:S(2)}, u32[]{:S(2)}) %all-to-all-start.9) | async-done | bytes 2097184 | tf_op jit(solution)/shard_map/all_to_all | solution.py:42
  1214.8 2.2 convolution_bitcast_fusion
  1217.0 64.6 %all-reduce.31.cloned.1.call-done = f32[128,256]{1,0:T(8,128)} async-done(((f32[128,256]{1,0:T(8,128)}), f32[128,256]{1,0:T(8,128)}) %all-reduce.31.cloned.1.call-update) | async-done | bytes 131088 | tf_op jit(solution)/shard_map/psum | solution.py:33
  1281.6 1.1 fusion.1
  (89 shorter events, 21.6 us)
Async XLA Ops:
  9.3 11.9 copy-start.3
  9.3 13.2 %copy-start.6 = (s32[1,5,6]{2,0,1:T(1,128)S(1)}, s32[1,5,6]{2,0,1:T(1,128)}, u32[]{:S(2)}) copy-start(s32[1,5,6]{2,0,1:T(1,128)} %param.33) | copy-start | bytes 364
  9.3 13.2 %copy-start.7 = (s32[1,5,6]{2,0,1:T(1,128)S(1)}, s32[1,5,6]{2,0,1:T(1,128)}, u32[]{:S(2)}) copy-start(s32[1,5,6]{2,0,1:T(1,128)} %param.36) | copy-start | bytes 364
  9.3 59.3 %all-to-all-start = ((bf16[32,1,128,256]{3,2,1,0:T(8,128)(2,1)}), bf16[32,1,128,256]{3,2,1,0:T(8,128)(2,1)S(1)}, u32[]{:S(2)}, u32[]{:S(2)}) async-start(bf16[32,1,128,256]{3,2,1,0:T(8,128)(2,1)} %stack.51), calls=%async_computation | async-start | bytes 4194304 | tf_op jit(solution)/shard_map/all_to_all | solution.py:42
  21.1 114.7 %all-reduce.13.cloned.1.call-start = ((), (), s32[]{:S(2)}) async-start(), calls=%async_computation.10 | async-start | bytes 262144 | tf_op jit(solution)/shard_map/psum | solution.py:33
  68.6 67.2 %copy-start.1 = (bf16[1,6,256,256]{3,2,1,0:T(8,128)(2,1)S(1)}, bf16[1,6,256,256]{3,2,1,0:T(8,128)(2,1)}, u32[]{:S(2)}) copy-start(bf16[1,6,256,256]{3,2,1,0:T(8,128)(2,1)} %param.30) | copy-start | bytes 2359300
  68.6 67.2 %copy-start.2 = (bf16[1,6,128,256]{3,2,1,0:T(8,128)(2,1)S(1)}, bf16[1,6,128,256]{3,2,1,0:T(8,128)(2,1)}, u32[]{:S(2)}) copy-start(bf16[1,6,128,256]{3,2,1,0:T(8,128)(2,1)} %param.29) | copy-start | bytes 1179652
  138.5 56.2 %all-to-all-start.1 = ((bf16[32,1,128,256]{3,2,1,0:T(8,128)(2,1)}), bf16[32,1,128,256]{3,2,1,0:T(8,128)(2,1)}, u32[]{:S(2)}, u32[]{:S(2)}) async-start(bf16[32,1,128,256]{3,2,1,0:T(8,128)(2,1)} %stack.52), calls=%async_computation.1 | async-start | bytes 4194304 | tf_op jit(solution)/shard_map/all_to_all | solution.py:42
  148.8 114.4 %all-reduce.15.cloned.1.call-start = ((), (), s32[]{:S(2)}) async-start(), calls=%async_computation.11 | async-start | bytes 262144 | tf_op jit(solution)/shard_map/psum | solution.py:33
  265.8 56.2 %all-to-all-start.2 = ((bf16[32,1,128,256]{3,2,1,0:T(8,128)(2,1)}), bf16[32,1,128,256]{3,2,1,0:T(8,128)(2,1)}, u32[]{:S(2)}, u32[]{:S(2)}) async-start(bf16[32,1,128,256]{3,2,1,0:T(8,128)(2,1)} %stack.53), calls=%async_computation.2 | async-start | bytes 4194304 | tf_op jit(solution)/shard_map/all_to_all | solution.py:42
  276.0 114.4 %all-reduce.17.cloned.1.call-start = ((), (), s32[]{:S(2)}) async-start(), calls=%async_computation.12 | async-start | bytes 262144 | tf_op jit(solution)/shard_map/psum | solution.py:33
  393.1 56.2 %all-to-all-start.3 = ((bf16[32,1,128,256]{3,2,1,0:T(8,128)(2,1)}), bf16[32,1,128,256]{3,2,1,0:T(8,128)(2,1)}, u32[]{:S(2)}, u32[]{:S(2)}) async-start(bf16[32,1,128,256]{3,2,1,0:T(8,128)(2,1)} %stack.54), calls=%async_computation.3 | async-start | bytes 4194304 | tf_op jit(solution)/shard_map/all_to_all | solution.py:42
  403.3 114.4 %all-reduce.19.cloned.1.call-start = ((), (), s32[]{:S(2)}) async-start(), calls=%async_computation.13 | async-start | bytes 262144 | tf_op jit(solution)/shard_map/psum | solution.py:33
  520.4 56.2 %all-to-all-start.4 = ((bf16[32,1,128,256]{3,2,1,0:T(8,128)(2,1)}), bf16[32,1,128,256]{3,2,1,0:T(8,128)(2,1)}, u32[]{:S(2)}, u32[]{:S(2)}) async-start(bf16[32,1,128,256]{3,2,1,0:T(8,128)(2,1)} %stack.55), calls=%async_computation.4 | async-start | bytes 4194304 | tf_op jit(solution)/shard_map/all_to_all | solution.py:42
  530.6 115.2 %copy-start = (bf16[1,6,256,256]{3,2,1,0:T(8,128)(2,1)S(1)}, bf16[1,6,256,256]{3,2,1,0:T(8,128)(2,1)}, u32[]{:S(2)}) copy-start(bf16[1,6,256,256]{3,2,1,0:T(8,128)(2,1)} %param.31) | copy-start | bytes 2359300
  530.6 115.2 %all-reduce.21.cloned.1.call-start = ((), (), s32[]{:S(2)}) async-start(), calls=%async_computation.14 | async-start | bytes 262144 | tf_op jit(solution)/shard_map/psum | solution.py:33
  648.6 10.4 copy-start.4
  648.6 12.2 copy-start.9
  648.6 56.2 %all-to-all-start.5 = ((bf16[32,1,128,256]{3,2,1,0:T(8,128)(2,1)}), bf16[32,1,128,256]{3,2,1,0:T(8,128)(2,1)S(1)}, u32[]{:S(2)}, u32[]{:S(2)}) async-start(bf16[32,1,128,256]{3,2,1,0:T(8,128)(2,1)} %stack.56), calls=%async_computation.5 | async-start | bytes 4194304 | tf_op jit(solution)/shard_map/all_to_all | solution.py:42
  658.9 113.5 %all-reduce.23.cloned.1.call-start = ((), (), s32[]{:S(2)}) async-start(), calls=%async_computation.15 | async-start | bytes 262144 | tf_op jit(solution)/shard_map/psum | solution.py:33
  704.9 0.8 copy-start.10
  775.1 11.1 copy-start.8
  775.1 56.3 %all-to-all-start.6 = ((bf16[32,1,128,256]{3,2,1,0:T(8,128)(2,1)}), bf16[32,1,128,256]{3,2,1,0:T(8,128)(2,1)}, u32[]{:S(2)}, u32[]{:S(2)}) async-start(bf16[32,1,128,256]{3,2,1,0:T(8,128)(2,1)} %stack.57), calls=%async_computation.6 | async-start | bytes 4194304 | tf_op jit(solution)/shard_map/all_to_all | solution.py:42
  785.4 114.4 %all-reduce.25.cloned.1.call-start = ((), (), s32[]{:S(2)}) async-start(), calls=%async_computation.16 | async-start | bytes 262144 | tf_op jit(solution)/shard_map/psum | solution.py:33
  902.5 56.2 %all-to-all-start.7 = ((bf16[32,1,128,256]{3,2,1,0:T(8,128)(2,1)}), bf16[32,1,128,256]{3,2,1,0:T(8,128)(2,1)}, u32[]{:S(2)}, u32[]{:S(2)}) async-start(bf16[32,1,128,256]{3,2,1,0:T(8,128)(2,1)} %stack.58), calls=%async_computation.7 | async-start | bytes 4194304 | tf_op jit(solution)/shard_map/all_to_all | solution.py:42
  912.7 114.4 %all-reduce.27.cloned.1.call-start = ((), (), s32[]{:S(2)}) async-start(), calls=%async_computation.17 | async-start | bytes 262144 | tf_op jit(solution)/shard_map/psum | solution.py:33
  1029.8 56.2 %all-to-all-start.8 = ((bf16[32,1,128,256]{3,2,1,0:T(8,128)(2,1)}), bf16[32,1,128,256]{3,2,1,0:T(8,128)(2,1)}, u32[]{:S(2)}, u32[]{:S(2)}) async-start(bf16[32,1,128,256]{3,2,1,0:T(8,128)(2,1)} %stack.59), calls=%async_computation.8 | async-start | bytes 4194304 | tf_op jit(solution)/shard_map/all_to_all | solution.py:42
  1040.0 114.4 %all-reduce.29.cloned.1.call-start = ((), (), s32[]{:S(2)}) async-start(), calls=%async_computation.18 | async-start | bytes 262144 | tf_op jit(solution)/shard_map/psum | solution.py:33
  1157.0 56.2 %all-to-all-start.9 = ((bf16[32,1,128,256]{3,2,1,0:T(8,128)(2,1)}), bf16[32,1,128,256]{3,2,1,0:T(8,128)(2,1)}, u32[]{:S(2)}, u32[]{:S(2)}) async-start(bf16[32,1,128,256]{3,2,1,0:T(8,128)(2,1)} %stack.60), calls=%async_computation.9 | async-start | bytes 4194304 | tf_op jit(solution)/shard_map/all_to_all | solution.py:42
  1167.2 114.3 %all-reduce.31.cloned.1.call-start = ((), (), s32[]{:S(2)}) async-start(), calls=%async_computation.19 | async-start | bytes 262144 | tf_op jit(solution)/shard_map/psum | solution.py:33
  1282.8 0.7 copy-start.5
Sparse Core Ops, SparseCore 0:
  71.7 64.0 all-reduce.12
  198.6 64.4 all-reduce.14
  325.9 64.4 all-reduce.16
  453.2 64.4 all-reduce.18
  581.3 64.4 all-reduce.20
  708.0 64.3 all-reduce.22
  835.3 64.4 all-reduce.24
  962.6 64.4 all-reduce.26
  1089.9 64.4 all-reduce.28
  1217.1 64.4 all-reduce.30
